TPU v7x, 128 devices: a whole 4x4x4 slice. The times are simulated.
128 devices in a mesh: grp: 4 (over y), mem: 32 (over x, z, core).
Axes of the slice: x: 4, y: 4, z: 4, core: 2. Of those that a mesh axis runs over, the one named last changes fastest.
Arguments:
- pno: bfloat16 [4096, 512, 128], P(('grp', 'mem')), may hold values from -0.5 to 0.5
- amplitudes: bfloat16 [4096, 128, 128], P(('grp', 'mem')), may hold values from -6 to 6
- pno_count: int32 [4096], P(('grp', 'mem')), may hold values from 64 to 128
- pao_coupling: bfloat16 [512, 512], replicated, may hold values from -0.25 to 0.25
- row_owner: int32 [8192, 1], P(('grp', 'mem')), may hold values from 0 to 31; in each aligned block of 64 rows (0 to 63, 64 to 127, ...) at most 4 rows name the same one
- row_pair: int32 [8192], P(('grp', 'mem')), may hold values from 0 to 31
- row_target: int32 [8192], P(('grp', 'mem')), may hold values from 0 to 31
- row_coef: float32 [8192], P(('grp', 'mem')), may hold values from -6 to 6
- column_owner: int32 [2048, 1], P(('grp', 'mem')), may hold values from 0 to 3; in each aligned block of 16 rows (0 to 15, 16 to 31, ...) at most 8 rows name the same one
- column_pair: int32 [2048], P(('grp', 'mem')), may hold values from 0 to 31
- column_target: int32 [2048], P(('grp', 'mem')), may hold values from 0 to 31
- column_coef: float32 [2048], P(('grp', 'mem')), may hold values from -6 to 6
Outputs:
- coupling_residual: float32 [4096, 128, 128], P(('grp', 'mem'))
Inputs may be any that keep to these rules, and one draw needn't show every extreme that they name: `row_owner`: among one device's in-group couplings at most 4 name the same member index, and some device's rows reach it. `column_owner`: among one device's cross-group couplings at most 8 name the same group index, and some device's rows reach it.
All inputs are finite; a program needn't handle non-finite values.
Results may differ from a plain program's by a relative error of at most 0.0064.
Values may be sent and summed in bfloat16 or wider, within the bound.
A program may use at most 128 MiB of HBM per device.

v0:
```python
import jax
import jax.numpy as jnp
from jax import lax
from jax.sharding import PartitionSpec as P


def masked_blocks(pno, amplitudes, pno_count):
    width = pno.shape[2]
    live = jnp.arange(width, dtype=jnp.int32)[None, :] < pno_count[:, None]
    live_pno = jnp.where(live[:, None, :], pno, jnp.zeros((), pno.dtype))
    live_amp = jnp.where(
        live[:, :, None] & live[:, None, :], amplitudes, jnp.zeros((), amplitudes.dtype)
    )
    return (live_pno, live_amp)


def metric_blocks(live_pno, pao_coupling):
    mixed = jnp.einsum("kj,tkp->tjp", pao_coupling, live_pno, preferred_element_type=jnp.float32)
    return (live_pno.astype(jnp.float32) + mixed).astype(jnp.bfloat16)


def coupling_terms(metric_rows, source_pno, source_amp):
    intersection = jnp.einsum(
        "tkp,tkq->tpq", metric_rows, source_pno, preferred_element_type=jnp.float32
    ).astype(jnp.bfloat16)
    half = jnp.einsum(
        "tpq,tqr->tpr", intersection, source_amp, preferred_element_type=jnp.float32
    ).astype(jnp.bfloat16)
    return jnp.einsum("tpr,tsr->tps", half, intersection, preferred_element_type=jnp.float32)


def slot_layout(owner, peers, capacity):
    onehot = (owner[:, None] == jnp.arange(peers, dtype=jnp.int32)[None, :]).astype(jnp.int32)
    before = jnp.cumsum(onehot, axis=0) - onehot
    rank = jnp.sum(before * onehot, axis=1)
    return owner * capacity + rank


def pair_total(target, terms, pairs):
    onehot = (jnp.arange(pairs, dtype=jnp.int32)[:, None] == target[None, :]).astype(jnp.float32)
    return jnp.einsum("at,tps->aps", onehot, terms, precision=lax.Precision.HIGHEST)


def shards(
    pno,
    amplitudes,
    pno_count,
    pao_coupling,
    row_owner,
    row_pair,
    row_target,
    row_coef,
    column_owner,
    column_pair,
    column_target,
    column_coef,
):
    pairs, width_k, width_p = pno.shape
    members = lax.axis_size("mem")
    groups = lax.axis_size("grp")
    row_cap = max(2, 2 * row_pair.shape[0] // members)
    col_cap = max(2, 2 * column_pair.shape[0] // groups)
    live_pno, live_amp = masked_blocks(pno, amplitudes, pno_count)
    metric = metric_blocks(live_pno, pao_coupling)
    row_metric = metric[row_target]
    col_metric = metric[column_target]
    row_slot = slot_layout(row_owner[:, 0], members, row_cap)
    wanted = jnp.zeros((members * row_cap,), jnp.int32).at[row_slot].set(row_pair)
    asked = lax.all_to_all(
        wanted.reshape(members, row_cap), "mem", split_axis=0, concat_axis=0, tiled=True
    )
    flat = asked.reshape(-1)
    sent_pno = live_pno[flat].reshape(members, row_cap, width_k, width_p)
    sent_amp = live_amp[flat].reshape(members, row_cap, width_p, width_p)
    got_pno, got_amp = (
        lax.all_to_all(sent_pno, "mem", split_axis=0, concat_axis=0, tiled=True),
        lax.all_to_all(sent_amp, "mem", split_axis=0, concat_axis=0, tiled=True),
    )
    source_pno = got_pno.reshape(members * row_cap, width_k, width_p)[row_slot]
    source_amp = got_amp.reshape(members * row_cap, width_p, width_p)[row_slot]
    row_terms = coupling_terms(row_metric, source_pno, source_amp)
    row_terms = row_coef[:, None, None] * row_terms
    col_slot = slot_layout(column_owner[:, 0], groups, col_cap)
    wanted_cols = jnp.zeros((groups * col_cap,), jnp.int32).at[col_slot].set(column_pair)
    asked_cols = lax.all_to_all(
        wanted_cols.reshape(groups, col_cap), "grp", split_axis=0, concat_axis=0, tiled=True
    )
    flat_cols = asked_cols.reshape(-1)
    out_pno = live_pno[flat_cols].reshape(groups, col_cap, width_k, width_p)
    out_amp = live_amp[flat_cols].reshape(groups, col_cap, width_p, width_p)
    back_pno, back_amp = (
        lax.all_to_all(out_pno, "grp", split_axis=0, concat_axis=0, tiled=True),
        lax.all_to_all(out_amp, "grp", split_axis=0, concat_axis=0, tiled=True),
    )
    col_pno = back_pno.reshape(groups * col_cap, width_k, width_p)[col_slot]
    col_amp = back_amp.reshape(groups * col_cap, width_p, width_p)[col_slot]
    col_terms = column_coef[:, None, None] * coupling_terms(col_metric, col_pno, col_amp)
    return -(pair_total(row_target, row_terms, pairs) + pair_total(column_target, col_terms, pairs))


def solution(mesh):
    in_specs = (
        P(("grp", "mem"), None, None),
        P(("grp", "mem"), None, None),
        P(("grp", "mem")),
        P(),
        P(("grp", "mem"), None),
        P(("grp", "mem")),
        P(("grp", "mem")),
        P(("grp", "mem")),
        P(("grp", "mem"), None),
        P(("grp", "mem")),
        P(("grp", "mem")),
        P(("grp", "mem")),
    )
    out_specs = P(("grp", "mem"), None, None)
    return jax.shard_map(shards, mesh=mesh, in_specs=in_specs, out_specs=out_specs, check_vma=False)
```

profile of v0, /device:TPU:36, one launch (start us, length us, event | category | flops | bytes accessed | tf_op | source)
XLA Modules:
  0.0 495.1 jit_solution(9517275852635852489)
XLA Ops:
  3.7 4.5 all-to-all-start.3
  12.2 1.8 and_select_fusion
  14.7 8.0 %all-to-all-start = ((s32[32,1,4]{2,1,0:T(1,128)}), s32[32,1,4]{2,1,0:T(1,128)S(1)}, u32[]{:S(2)}, u32[]{:S(2)}) async-start(s32[32,1,4]{2,1,0:T(1,128)} %bitcast.6), calls=%async_computation | async-start | bytes 32768 | tf_op jit(solution)/shard_map/all_to_all | solution.py:69
  23.9 1.7 gather_fusion.8
  25.6 1.5 all-to-all-done
  27.1 4.8 all-to-all-start.5
  31.9 6.4 %copy.19 = bf16[32,512,128]{1,2,0:T(8,128)(2,1)} copy(bf16[32,512,128]{2,1,0:T(8,128)(2,1)} %param.12) | data formatting | bytes 8388608 | tf_op args[0]
  38.3 3.9 broadcast_select_fusion
  42.2 4.9 gather_fusion.6
  48.1 4.8 all-to-all-start.4
  53.8 3.1 gather_fusion.3
  56.9 45.0 %all-to-all-done.4 = bf16[4,8,512,128]{2,3,1,0:T(8,128)(2,1)} async-done(((bf16[4,8,512,128]{2,3,1,0:T(8,128)(2,1)}), bf16[4,8,512,128]{2,3,1,0:T(8,128)(2,1)}, u32[]{:S(2)}, u32[]{:S(2)}) %all-to-all-start.4) | async-done | bytes 4194336 | tf_op jit(solution)/shard_map/all_to_all | solution.py:92
  101.9 7.7 %all-to-all-start.2 = ((bf16[32,4,128,128]{3,2,1,0:T(8,128)(2,1)}), bf16[32,4,128,128]{3,2,1,0:T(8,128)(2,1)}, u32[]{:S(2)}, u32[]{:S(2)}) async-start(bf16[32,4,128,128]{3,2,1,0:T(8,128)(2,1)} %bitcast.55), calls=%async_computation.2 | async-start | bytes 8388608 | tf_op jit(solution)/shard_map/all_to_all | solution.py:77
  109.6 10.2 %gather_fusion.1 = bf16[128,512,128]{1,2,0:T(8,128)(2,1)} fusion(bf16[32,512,128]{1,2,0:T(8,128)(2,1)} %broadcast_select_fusion, s32[1024]{0:T(1024)S(1)} %pad_clamp_fusion.4), kind=kCustom, calls=%fused_computation.1 | custom fusion | bytes 33554944 | tf_op jit(solution)/shard_map/gather | solution.py:73
  119.8 40.0 %all-to-all-done.2 = bf16[32,4,128,128]{3,2,1,0:T(8,128)(2,1)} async-done(((bf16[32,4,128,128]{3,2,1,0:T(8,128)(2,1)}), bf16[32,4,128,128]{3,2,1,0:T(8,128)(2,1)}, u32[]{:S(2)}, u32[]{:S(2)}) %all-to-all-start.2) | async-done | bytes 4194336 | tf_op jit(solution)/shard_map/all_to_all | solution.py:77
  159.8 9.2 %all-to-all-start.1 = ((bf16[32,4,512,128]{2,3,1,0:T(8,128)(2,1)}), bf16[32,4,512,128]{2,3,1,0:T(8,128)(2,1)}, u32[]{:S(2)}, u32[]{:S(2)}) async-start(bf16[32,4,512,128]{2,3,1,0:T(8,128)(2,1)} %bitcast.52), calls=%async_computation.1 | async-start | bytes 33554432 | tf_op jit(solution)/shard_map/all_to_all | solution.py:76
  169.0 7.8 %fusion = bf16[32,512,128]{1,2,0:T(8,128)(2,1)} fusion(bf16[32,512,128]{1,2,0:T(8,128)(2,1)} %broadcast_select_fusion, bf16[512,512]{1,0:T(8,128)(2,1)S(1)} %copy-done), kind=kOutput, calls=%fused_computation.13 | convolution fusion | flops 2153775104 | bytes 8912896 | tf_op jit(solution)/shard_map/kj,tkp->tjp/dot_general | solution.py:18
  176.9 7.7 %gather_fusion = bf16[64,512,128]{1,2,0:T(8,128)(2,1)} fusion(bf16[32,512,128]{1,2,0:T(8,128)(2,1)} %fusion, s32[1024]{0:T(1024)S(1)} %pad_clamp_fusion.5), kind=kCustom, calls=%fused_computation | custom fusion | bytes 16777472 | tf_op jit(solution)/shard_map/gather | solution.py:65
  184.6 2.9 gather_fusion.5
  187.5 1.9 gather_fusion.9
  189.4 6.2 %copy.24 = bf16[4,8,512,128]{3,2,1,0:T(8,128)(2,1)} copy(bf16[4,8,512,128]{2,3,1,0:T(8,128)(2,1)} %all-to-all-done.4) | data formatting | bytes 8388608 | tf_op jit(solution)/shard_map/all_to_all | solution.py:92
  195.6 4.3 gather_fusion.7
  199.9 2.3 convolution_convert_fusion.1
  202.9 2.9 fusion.10
  205.7 4.4 gather_fusion.4
  210.1 227.8 %all-to-all-done.1 = bf16[32,4,512,128]{2,3,1,0:T(8,128)(2,1)} async-done(((bf16[32,4,512,128]{2,3,1,0:T(8,128)(2,1)}), bf16[32,4,512,128]{2,3,1,0:T(8,128)(2,1)}, u32[]{:S(2)}, u32[]{:S(2)}) %all-to-all-start.1) | async-done | bytes 16777248 | tf_op jit(solution)/shard_map/all_to_all | solution.py:76
  437.9 22.5 %copy.21 = bf16[32,4,512,128]{3,2,1,0:T(8,128)(2,1)} copy(bf16[32,4,512,128]{2,3,1,0:T(8,128)(2,1)} %all-to-all-done.1) | data formatting | bytes 33554432 | tf_op jit(solution)/shard_map/all_to_all | solution.py:76
  460.4 11.3 %gather_fusion.2 = bf16[64,512,128]{2,1,0:T(8,128)(2,1)} fusion(bf16[128,512,128]{2,1,0:T(8,128)(2,1)} %bitcast.53, s32[1024]{0:T(1024)S(1)} %pad_clamp_fusion.3), kind=kCustom, calls=%fused_computation.2 | custom fusion | bytes 16777472 | tf_op jit(solution)/shard_map/gather | solution.py:79
  471.8 8.1 %fusion.29 = bf16[64,128,128]{2,1,0:T(8,128)(2,1)S(1)} fusion(bf16[64,512,128]{1,2,0:T(8,128)(2,1)} %gather_fusion, bf16[64,512,128]{2,1,0:T(8,128)(2,1)} %gather_fusion.2), kind=kOutput, calls=%fused_computation.64 | convolution fusion | flops 1073741824 | bytes 18874368 | tf_op jit(solution)/shard_map/tkp,tkq->tpq/dot_general | solution.py:23
  479.9 5.7 %convolution_multiply_fusion = f32[64,128,128]{2,1,0:T(8,128)} fusion(bf16[64,128,128]{2,1,0:T(8,128)(2,1)} %gather_fusion.4, bf16[64,128,128]{2,1,0:T(8,128)(2,1)S(1)} %fusion.29, f32[64]{0:T(128)S(1)} %copy-done.6), kind=kOutput, calls=%fused_computation.17 | convolution fusion | flops 538968064 | bytes 8388864 | tf_op jit(solution)/shard_map/tpr,tsr->tps/dot_general | solution.py:29
  485.6 7.0 %add_negate_fusion = f32[32,128,128]{2,0,1:T(8,128)S(1)} fusion(f32[32,128,128]{2,0,1:T(8,128)} %fusion.10, f32[64,128,128]{2,1,0:T(8,128)} %convolution_multiply_fusion, s32[64]{0:T(128)S(1)} %copy-done.3), kind=kOutput, calls=%fused_computation.18 | convolution fusion | flops 403703808 | bytes 8388864 | tf_op jit(solution)/shard_map/at,tps->aps/dot_general | solution.py:41
  492.6 2.5 copy.26
  (45 shorter events, 12.1 us)
Async XLA Ops:
  0.0 169.0 %copy-start = (bf16[512,512]{1,0:T(8,128)(2,1)S(1)}, bf16[512,512]{1,0:T(8,128)(2,1)}, u32[]{:S(2)}) copy-start(bf16[512,512]{1,0:T(8,128)(2,1)} %param.15) | copy-start | bytes 1572868
  3.7 10.9 %all-to-all-start.3 = ((s32[4,1,8]{2,1,0:T(1,128)}), s32[4,1,8]{2,1,0:T(1,128)S(1)}, u32[]{:S(2)}, u32[]{:S(2)}) async-start(s32[4,1,8]{2,1,0:T(1,128)} %bitcast.16), calls=%async_computation.3 | async-start | bytes 4096 | tf_op jit(solution)/shard_map/all_to_all | solution.py:85
  14.7 12.4 %all-to-all-start = ((s32[32,1,4]{2,1,0:T(1,128)}), s32[32,1,4]{2,1,0:T(1,128)S(1)}, u32[]{:S(2)}, u32[]{:S(2)}) async-start(s32[32,1,4]{2,1,0:T(1,128)} %bitcast.6), calls=%async_computation | async-start | bytes 32768 | tf_op jit(solution)/shard_map/all_to_all | solution.py:69
  27.1 20.1 %all-to-all-start.5 = ((bf16[4,8,128,128]{3,2,1,0:T(8,128)(2,1)}), bf16[4,8,128,128]{3,2,1,0:T(8,128)(2,1)S(1)}, u32[]{:S(2)}, u32[]{:S(2)}) async-start(bf16[4,8,128,128]{3,2,1,0:T(8,128)(2,1)} %bitcast.20), calls=%async_computation.5 | async-start | bytes 2097152 | tf_op jit(solution)/shard_map/all_to_all | solution.py:93
  47.1 1.0 copy-start.2
  48.1 53.8 %all-to-all-start.4 = ((bf16[4,8,512,128]{2,3,1,0:T(8,128)(2,1)}), bf16[4,8,512,128]{2,3,1,0:T(8,128)(2,1)}, u32[]{:S(2)}, u32[]{:S(2)}) async-start(bf16[4,8,512,128]{2,3,1,0:T(8,128)(2,1)} %bitcast.54), calls=%async_computation.4 | async-start | bytes 8388608 | tf_op jit(solution)/shard_map/all_to_all | solution.py:92
  101.9 57.9 %all-to-all-start.2 = ((bf16[32,4,128,128]{3,2,1,0:T(8,128)(2,1)}), bf16[32,4,128,128]{3,2,1,0:T(8,128)(2,1)}, u32[]{:S(2)}, u32[]{:S(2)}) async-start(bf16[32,4,128,128]{3,2,1,0:T(8,128)(2,1)} %bitcast.55), calls=%async_computation.2 | async-start | bytes 8388608 | tf_op jit(solution)/shard_map/all_to_all | solution.py:77
  159.8 9.2 %copy-start.3 = (s32[64]{0:T(128)S(1)}, s32[64]{0:T(128)}, u32[]{:S(2)}) copy-start(s32[64]{0:T(128)} %param.18) | copy-start | bytes 772
  159.8 278.1 %all-to-all-start.1 = ((bf16[32,4,512,128]{2,3,1,0:T(8,128)(2,1)}), bf16[32,4,512,128]{2,3,1,0:T(8,128)(2,1)}, u32[]{:S(2)}, u32[]{:S(2)}) async-start(bf16[32,4,512,128]{2,3,1,0:T(8,128)(2,1)} %bitcast.52), calls=%async_computation.1 | async-start | bytes 33554432 | tf_op jit(solution)/shard_map/all_to_all | solution.py:76
  176.9 7.7 %copy-start.5 = (s32[16]{0:T(128)S(1)}, s32[16]{0:T(128)}, u32[]{:S(2)}) copy-start(s32[16]{0:T(128)} %param.22) | copy-start | bytes 196
  195.6 6.6 %copy-start.4 = (f32[16]{0:T(128)S(1)}, f32[16]{0:T(128)}, u32[]{:S(2)}) copy-start(f32[16]{0:T(128)} %param.23) | copy-start | bytes 196
  471.8 8.1 %copy-start.6 = (f32[64]{0:T(128)S(1)}, f32[64]{0:T(128)}, u32[]{:S(2)}) copy-start(f32[64]{0:T(128)} %param.19) | copy-start | bytes 772
  485.6 9.5 %copy-start.1 = (bf16[512,512]{1,0:T(8,128)(2,1)S(1)}, bf16[512,512]{1,0:T(8,128)(2,1)}, u32[]{:S(2)}) copy-start(bf16[512,512]{1,0:T(8,128)(2,1)} %param.15) | copy-start | bytes 1572868
where the time goes:
time: 497 us; the launch traced here: 495 us
  waiting for transfers between devices  314 us (63%)
  local copies, waits for them, and re-layouts  94.7 us (19%)
  starting transfers between devices  39 us (8%)
  matrix products  34.4 us (7%)
  other arithmetic  12.4 us (2%)
    all_to_all x1, waiting for transfers between devices, shards(): lax.all_to_all(sent_pno, 'mem', split_axis=0, concat_axis=0, tiled=True)  228 us
    all_to_all x1, waiting for transfers between devices, shards(): lax.all_to_all(out_pno, 'grp', split_axis=0, concat_axis=0, tiled=True)  45 us
    all_to_all x1, waiting for transfers between devices, shards(): lax.all_to_all(sent_amp, 'mem', split_axis=0, concat_axis=0, tiled=True)  40 us
    all_to_all x1, local copies, waits for them, and re-layouts, shards(): lax.all_to_all(sent_pno, 'mem', split_axis=0, concat_axis=0, tiled=True)  22.5 us
    gather x1, local copies, waits for them, and re-layouts, shards(): source_pno = got_pno.reshape(members * row_cap, width_k, width_p)[row_slot]  11.3 us
    dot_general x2, matrix products, coupling_terms(): jnp.einsum('tkp,tkq->tpq', metric_rows, source_pno, preferred_element_typ...  10.4 us
    gather x1, local copies, waits for them, and re-layouts, shards(): sent_pno = live_pno[flat].reshape(members, row_cap, width_k, width_p)  10.2 us
  transfers between devices with their start and end apart: 6, of which 4 were waited for; matrix products, arithmetic and copies ran while one was open for 16% of the time, Pallas kernels for 0%

commit v1 on v0

v1 whole, which is shorter than its diff:
```python
import functools

import jax
import jax.numpy as jnp
from jax import lax
from jax.experimental import pallas as pl
from jax.experimental.pallas import tpu as pltpu
from jax.sharding import PartitionSpec as P

MESH = pl.DeviceIdType.MESH
HALF = 16


def gather_kernel(
    pno, amp, ints, flts, mix,
    row_l, row_a, z_l, y_l, y_a, ints_in, flts_in, met,
    mix_v, send_sem, recv_sem,
):
    me = lax.axis_index("mem")
    g = lax.axis_index("grp")
    core = me % 2
    z = (me // 2) % 4
    x = me // 8

    def at(dx, dz, dc):
        nx = (x + dx) % 4
        nz = (z + dz) % 4
        nc = (core + dc) % 2
        return (g, nx * 8 + nz * 2 + nc)

    def up(dg):
        return ((g + dg) % 4, me)

    row = [at(1, 0, 0), at(3, 0, 0), at(2, 0, 0), at(0, 0, 1), at(1, 0, 1), at(3, 0, 1), at(2, 0, 1)]
    col = [at(0, 1, 0), at(0, 3, 0), at(0, 2, 0)]
    tall = [up(1), up(3), up(2)]
    back = {0: 1, 1: 0, 2: 2, 3: 3, 4: 5, 5: 4, 6: 6}

    barrier = pltpu.get_barrier_semaphore()
    peers = row + col + tall
    for d in peers:
        pl.semaphore_signal(barrier, inc=1, device_id=d, device_id_type=MESH)
    pl.semaphore_wait(barrier, len(peers))

    count = [0]
    live = []

    def send(src, dst, dev):
        i = count[0]
        count[0] += 1
        cp = pltpu.make_async_remote_copy(
            src_ref=src, dst_ref=dst, send_sem=send_sem.at[i], recv_sem=recv_sem.at[i],
            device_id=dev, device_id_type=MESH,
        )
        cp.start()
        live.append(cp)
        return cp

    H1 = pl.ds(0, HALF)
    H2 = pl.ds(HALF, HALF)

    def own(dsts, srcs, devs):
        res = {}
        for way, first, second in ((0, H2, H1), (1, H1, H2)):
            slot = 1 - way
            for name, h in (("first", first), ("second", second)):
                for src, dst in zip(srcs, dsts):
                    res.setdefault((slot, name), []).append(
                        send(src.at[h], dst.at[slot, h], devs[way])
                    )
        return res

    for k, d in enumerate(row):
        send(ints, ints_in.at[back[k]], d)
    for k, d in enumerate(col):
        send(ints, ints_in.at[7 + back[k]], d)
        send(flts, flts_in.at[back[k]], d)
    for k, d in enumerate(tall):
        send(ints, ints_in.at[10 + back[k]], d)

    got_z = own([z_l], [pno], col)
    got_x = own([row_l, row_a], [pno, amp], row)
    got_y = own([y_l, y_a], [pno, amp], tall)
    mate = row[3]
    send(pno, row_l.at[3], mate)
    send(amp, row_a.at[3], mate)

    pltpu.sync_copy(mix, mix_v)

    def metric_of(src, dst):
        def body(l_ref, m_ref):
            for u in range(0, 4, 2):
                two = jnp.concatenate([l_ref[u], l_ref[u + 1]], axis=1)
                mixed = jnp.dot(mix_v[...], two, preferred_element_type=jnp.float32)
                full = (two.astype(jnp.float32) + mixed).astype(jnp.bfloat16)
                m_ref[u] = full[:, :128].T
                m_ref[u + 1] = full[:, 128:].T

        pltpu.emit_pipeline(
            body, grid=(8,),
            in_specs=[pl.BlockSpec((4, 512, 128), lambda i: (i, 0, 0))],
            out_specs=[pl.BlockSpec((4, 128, 512), lambda i: (i, 0, 0))],
        )(src, dst)

    metric_of(pno, met.at[0])

    def relay(got, dsts, devs, to_mate):
        out = []
        for slot, h, way in ((1, H2, 0), (0, H1, 1)):
            for cp in got[(slot, "first")]:
                cp.wait_recv()
            for dst in dsts:
                out.append(send(dst.at[slot, h], dst.at[2, h], devs[way]))
            if to_mate:
                for dst in dsts:
                    send(dst.at[slot, h], dst.at[4 + slot, h], mate)
        return out

    far_z = relay(got_z, [z_l], col, False)
    far_x = relay(got_x, [row_l, row_a], row, True)
    far_y = relay(got_y, [y_l, y_a], tall, False)
    for slot in (0, 1):
        for cp in got_z[(slot, "second")]:
            cp.wait_recv()
        metric_of(z_l.at[slot], met.at[1 + slot])
    for slot, h in ((1, H1), (0, H2)):
        for cp in got_x[(slot, "second")]:
            cp.wait_recv()
        for dst in (row_l, row_a):
            send(dst.at[slot, h], dst.at[4 + slot, h], mate)
    for cp in far_z:
        cp.wait_recv()
    metric_of(z_l.at[2], met.at[3])
    for k, h in ((0, H2), (1, H1)):
        for cp in far_x[2 * k:2 * k + 2]:
            cp.wait_recv()
        for dst in (row_l, row_a):
            send(dst.at[2, h], dst.at[6, h], mate)
    waited = set()
    for got in (got_z, got_x):
        for cps in got.values():
            waited.update(id(cp) for cp in cps)
    for slot in (0, 1):
        waited.update(id(cp) for cp in got_y[(slot, "first")])
    waited.update(id(cp) for cp in far_z + far_x)
    for cp in live:
        cp.wait_send()
        if id(cp) not in waited:
            cp.wait_recv()


N_COPY = 17 + 3 + 4 + 8 + 8 + 2 + 2 + 8 + 4 + 4 + 4 - 1


def gather(pno, amp, ints, flts, mix):
    bf = jnp.bfloat16
    any_spec = pl.BlockSpec(memory_space=pl.ANY)
    outs = [
        jax.ShapeDtypeStruct((7, 32, 512, 128), bf),
        jax.ShapeDtypeStruct((7, 32, 128, 128), bf),
        jax.ShapeDtypeStruct((3, 32, 512, 128), bf),
        jax.ShapeDtypeStruct((3, 32, 512, 128), bf),
        jax.ShapeDtypeStruct((3, 32, 128, 128), bf),
        jax.ShapeDtypeStruct((13, 8, 128), jnp.int32),
        jax.ShapeDtypeStruct((3, 8, 128), jnp.float32),
        jax.ShapeDtypeStruct((4, 32, 128, 512), bf),
    ]
    return pl.pallas_call(
        gather_kernel,
        out_shape=outs,
        in_specs=[any_spec] * 5,
        out_specs=[any_spec] * 8,
        scratch_shapes=[
            pltpu.VMEM((512, 512), bf),
            pltpu.SemaphoreType.DMA((72,)),
            pltpu.SemaphoreType.DMA((72,)),
        ],
        compiler_params=pltpu.CompilerParams(collective_id=0, has_side_effects=True),
    )(pno, amp, ints, flts, mix)


UNROLL = 4
DEPTH = 2


def task_kernel(
    ints, ints_in, flts, flts_in,
    pno, amp, row_l, row_a, y_l, y_a, met,
    own_out, far_out,
    acc, l_buf, a_buf, m_buf, t_list, s_list, p_list, q_list, c_list, sem,
):
    me = lax.axis_index("mem")
    g = lax.axis_index("grp")
    core = me % 2
    z = (me // 2) % 4
    x = me // 8

    def int_of(slot, r, c):
        return ints_in[slot, r, c]

    def put(n, keep, target, slot, pair, live_p, live_q, coef):
        t_list[n] = target
        s_list[n] = slot * 32 + pair
        p_list[n] = live_p
        q_list[n] = live_q
        c_list[n] = -coef
        return n + keep

    n = jnp.int32(0)
    for td in range(4):
        def step(t, n, td=td):
            if td == 0:
                owner, pair, target = ints[0, t], ints[0, 64 + t], ints[1, t]
                coef = flts[0, t]
                live_p = ints[1, 64 + target]
            else:
                k = 6 + td
                owner, pair, target = ints_in[k, 0, t], ints_in[k, 0, 64 + t], ints_in[k, 1, t]
                coef = flts_in[td - 1, 0, t]
                live_p = ints_in[k, 1, 64 + target]
            keep = (((owner // 2) % 4) == z).astype(jnp.int32)
            dx = (owner // 8 - x + 4) % 4
            rel = jnp.where(dx == 1, 0, jnp.where(dx == 3, 1, 2))
            same = (owner % 2) == core
            slot = jnp.where(dx == 0, jnp.where(same, 7, 3), jnp.where(same, rel, 4 + rel))
            far = jnp.minimum(slot, 6)
            live_q = jnp.where(slot == 7, ints[1, 64 + pair], ints_in[far, 1, 64 + pair])
            return put(n, keep, td * 32 + target, slot, pair, live_p, live_q, coef)

        n = lax.fori_loop(0, 64, step, n)

    def col_step(t, n):
        owner, pair, target = ints[2, t], ints[2, 16 + t], ints[2, 32 + t]
        coef = flts[0, 64 + t]
        dg = (owner - g + 4) % 4
        rel = jnp.where(dg == 1, 0, jnp.where(dg == 3, 1, 2))
        slot = jnp.where(dg == 0, 7, 8 + rel)
        live_q = jnp.where(dg == 0, ints[1, 64 + pair], ints_in[10 + rel, 1, 64 + pair])
        return put(n, 1, target, slot, pair, ints[1, 64 + target], live_q, coef)

    n = lax.fori_loop(0, 16, col_step, n)
    for u in range(UNROLL):
        put(n + u, 0, 0, 7, 0, 0, 0, jnp.float32(0))
    steps = (n + UNROLL - 1) // UNROLL

    def copies(i, b):
        for u in range(UNROLL):
            k = i * UNROLL + u
            code = s_list[k]
            slot, pair = code // 32, code % 32
            target = t_list[k]
            yield u, slot, pair, target // 32, target % 32

    def start(i, b):
        for u, slot, pair, td, tp in copies(i, b):
            pltpu.make_async_copy(met.at[td, tp], m_buf.at[b, u], sem.at[b, u, 2]).start()

            @pl.when(slot < 7)
            def _():
                pltpu.make_async_copy(row_l.at[slot, pair], l_buf.at[b, u], sem.at[b, u, 0]).start()
                pltpu.make_async_copy(row_a.at[slot, pair], a_buf.at[b, u], sem.at[b, u, 1]).start()

            @pl.when(slot == 7)
            def _():
                pltpu.make_async_copy(pno.at[pair], l_buf.at[b, u], sem.at[b, u, 0]).start()
                pltpu.make_async_copy(amp.at[pair], a_buf.at[b, u], sem.at[b, u, 1]).start()

            @pl.when(slot > 7)
            def _():
                pltpu.make_async_copy(y_l.at[slot - 8, pair], l_buf.at[b, u], sem.at[b, u, 0]).start()
                pltpu.make_async_copy(y_a.at[slot - 8, pair], a_buf.at[b, u], sem.at[b, u, 1]).start()

    def wait(b):
        for u in range(UNROLL):
            pltpu.make_async_copy(met.at[0, 0], m_buf.at[b, u], sem.at[b, u, 2]).wait()
            pltpu.make_async_copy(pno.at[0], l_buf.at[b, u], sem.at[b, u, 0]).wait()
            pltpu.make_async_copy(amp.at[0], a_buf.at[b, u], sem.at[b, u, 1]).wait()

    start(0, 0)
    acc[...] = jnp.zeros_like(acc)
    rows = lax.broadcasted_iota(jnp.int32, (128, 128), 0)
    lanes = lax.broadcasted_iota(jnp.int32, (128, 128), 1)

    def step(i, carry):
        b = i % 2
        wait(b)

        @pl.when(i + 1 < steps)
        def _():
            start(i + 1, 1 - b)

        terms = []
        for u in range(UNROLL):
            k = i * UNROLL + u
            inter = jnp.dot(m_buf[b, u], l_buf[b, u], preferred_element_type=jnp.float32)
            keep = (rows < p_list[k]) & (lanes < q_list[k])
            terms.append(jnp.where(keep, inter, 0.0).astype(jnp.bfloat16))
        halves = [
            jnp.dot(terms[u], a_buf[b, u], preferred_element_type=jnp.float32).astype(jnp.bfloat16)
            for u in range(UNROLL)
        ]
        for u in range(UNROLL):
            k = i * UNROLL + u
            term = lax.dot_general(
                halves[u], terms[u], (((1,), (1,)), ((), ())), preferred_element_type=jnp.float32
            )
            t = t_list[k]
            acc[t] = acc[t] + c_list[k] * term
        return carry

    lax.fori_loop(0, steps, step, 0)
    own_out[...] = acc[0:32]
    far_out[...] = acc[32:128].astype(jnp.bfloat16)


def tasks(ints, ints_in, flts, flts_in, pno, amp, row_l, row_a, y_l, y_a, met):
    bf = jnp.bfloat16
    any_spec = pl.BlockSpec(memory_space=pl.ANY)
    smem = pl.BlockSpec(memory_space=pltpu.SMEM)
    vmem = pl.BlockSpec(memory_space=pltpu.VMEM)
    size = 256 + 16 + UNROLL
    return pl.pallas_call(
        task_kernel,
        out_shape=[
            jax.ShapeDtypeStruct((32, 128, 128), jnp.float32),
            jax.ShapeDtypeStruct((96, 128, 128), bf),
        ],
        in_specs=[smem] * 4 + [any_spec] * 7,
        out_specs=[vmem, vmem],
        scratch_shapes=[
            pltpu.VMEM((128, 128, 128), jnp.float32),
            pltpu.VMEM((2, UNROLL, 512, 128), bf),
            pltpu.VMEM((2, UNROLL, 128, 128), bf),
            pltpu.VMEM((2, UNROLL, 128, 512), bf),
            pltpu.SMEM((size,), jnp.int32),
            pltpu.SMEM((size,), jnp.int32),
            pltpu.SMEM((size,), jnp.int32),
            pltpu.SMEM((size,), jnp.int32),
            pltpu.SMEM((size,), jnp.float32),
            pltpu.SemaphoreType.DMA((2, UNROLL, 3)),
        ],
        compiler_params=pltpu.CompilerParams(vmem_limit_bytes=40 << 20),
    )(ints, ints_in, flts, flts_in, pno, amp, row_l, row_a, y_l, y_a, met)


def shards(
    pno, amplitudes, pno_count, pao_coupling,
    row_owner, row_pair, row_target, row_coef,
    column_owner, column_pair, column_target, column_coef,
):
    zeros = functools.partial(jnp.zeros, dtype=jnp.int32)
    ints = jnp.concatenate([
        row_owner[:, 0], row_pair, row_target, pno_count, zeros((32,)),
        column_owner[:, 0], column_pair, column_target, zeros((80 + 5 * 128,)),
    ]).reshape(8, 128)
    flts = jnp.concatenate(
        [row_coef, column_coef, jnp.zeros((48 + 7 * 128,), jnp.float32)]
    ).reshape(8, 128)
    row_l, row_a, z_l, y_l, y_a, ints_in, flts_in, met = gather(
        pno, amplitudes, ints, flts, pao_coupling.T
    )
    own, far = tasks(ints, ints_in, flts, flts_in, pno, amplitudes, row_l, row_a, y_l, y_a, met)

    def moved(part, dz):
        perm = []
        for m in range(32):
            x, z, c = m // 8, (m // 2) % 4, m % 2
            perm.append((m, x * 8 + ((z + dz) % 4) * 2 + c))
        return lax.ppermute(part, "mem", perm).astype(jnp.float32)

    return own + moved(far[0:32], 1) + moved(far[32:64], 3) + moved(far[64:96], 2)


def solution(mesh):
    both = P(("grp", "mem"))
    in_specs = (
        P(("grp", "mem"), None, None),
        P(("grp", "mem"), None, None),
        both,
        P(),
        P(("grp", "mem"), None),
        both,
        both,
        both,
        P(("grp", "mem"), None),
        both,
        both,
        both,
    )
    out_specs = P(("grp", "mem"), None, None)
    return jax.shard_map(shards, mesh=mesh, in_specs=in_specs, out_specs=out_specs, check_vma=False)
```

time: 497 us -> 293 us (0.59)
  the two profiles are of different devices: /device:TPU:36 before, /device:TPU:1 now
where the time goes in v1:
time: 293 us; the launch traced here: 292 us
  Pallas kernels  230 us (78%)
  waiting for transfers between devices  45 us (15%)
  local copies, waits for them, and re-layouts  9.43 us (3%)
  starting transfers between devices  4.17 us (1%)
  other arithmetic  3.42 us (1%)
    pallas_call x1, Pallas kernels, gather(): pl.pallas_call(gather_kernel, out_shape=outs, in_specs=[any_spec] * 5, ou...  188 us
    ppermute x3, waiting for transfers between devices, moved(): return lax.ppermute(part, 'mem', perm).astype(jnp.float32)  45 us
    pallas_call x1, Pallas kernels, tasks(): pl.pallas_call(task_kernel, out_shape=[jax.ShapeDtypeStruct((32, 128, 128...  42.5 us
    unnamed x15, local copies, waits for them, and re-layouts  7.64 us
  transfers between devices with their start and end apart: 3, of which 2 were waited for; matrix products, arithmetic and copies ran while one was open for 0% of the time, Pallas kernels for 0%

profile of v1, /device:TPU:1, one launch (start us, length us, event | category | flops | bytes accessed | tf_op | source)
XLA Modules:
  0.0 292.3 jit_solution(16803578617650822666)
XLA Ops:
  0.0 2.0 copy.13
  2.0 0.0 copy-start.1
  2.1 1.4 maximum_bitcast_fusion.flts
  3.5 0.0 copy-start.5
  3.5 1.4 concatenate.6
  4.9 0.0 copy-start.4
  4.9 187.7 %shard_map.118 = (bf16[7,32,512,128]{3,2,1,0:T(8,128)(2,1)}, bf16[7,32,128,128]{3,2,1,0:T(8,128)(2,1)}, bf16[3,32,512,128]{3,2,1,0:T(8,128)(2,1)}, bf16[3,32,512...) custom-call(bf16[32,512,128]{2,1,0:T(8,128)(2,1)} %pno.3, ...), custom_call_target="tpu_custom_call" | custom-call | tf_op jit(solution)/shard_map/pallas_call | solution.py:168
  192.6 0.0 copy-done.1
  192.7 0.0 copy-done.5
  192.7 0.0 copy-done.4
  192.7 0.0 copy-start
  192.7 2.2 copy-done
  194.9 0.0 copy-start.2
  194.9 1.9 copy-done.2
  196.8 0.0 copy-start.3
  196.8 0.8 copy-done.3
  197.6 0.0 copy-start.6
  197.6 0.7 copy-done.6
  198.3 42.5 %shard_map.119 = (f32[32,128,128]{2,1,0:T(8,128)S(1)}, bf16[96,128,128]{2,1,0:T(8,128)(2,1)S(1)}) custom-call(s32[8,128]{1,0:T(8,128)S(1)} %bitcast.7, s32[13,8,128]{2,1,0:T(8,128)S(1)} %copy-done.3, f32[8,128]{1,0:T(8,128)S(1)} %copy-done.5, f32[3,8,128]{2,1,0:T(8,128)S(1)} %copy-done.6, bf16[32,512,128]{2,1,0:T(8,128)(2,1)S(1)} %copy-done, ...), custom_call_target="tpu_custom_call" | custom-call | tf_op jit(solution)/shard_map/pallas_call | solution.py:322
  240.8 0.4 fusion
  241.2 0.1 collective-permute-start
  241.3 4.1 %collective-permute-start.2 = (bf16[32,128,128]{2,1,0:T(8,128)(2,1)S(1)}, bf16[32,128,128]{2,1,0:T(8,128)(2,1)S(1)}, u32[]{:S(2)}, u32[]{:S(2)}) collective-permute-start(bf16[32,128,128]{2,1,0:T(8,128)(2,1)S(1)} %get-tuple-element.24), channel_id=1, source_target_pairs={{0,4},{1,5},{2,6},{3,7},{4,0},{5,1},{6,2},{7,3},{8,12},{9,13},{10,... | collective-permute-start | bytes 3145736 | tf_op jit(solution)/shard_map/ppermute | solution.py:369
  245.4 0.0 collective-permute-start.1
  245.4 21.6 %collective-permute-done = bf16[32,128,128]{2,1,0:T(8,128)(2,1)S(1)} collective-permute-done((bf16[32,128,128]{2,1,0:T(8,128)(2,1)S(1)}, bf16[32,128,128]{2,1,0:T(8,128)(2,1)S(1)}, u32[]{:S(2)}, u32[]{:S(2)}) %collective-permute-start) | collective-permute-done | bytes 1048608 | tf_op jit(solution)/shard_map/ppermute | solution.py:369
  267.0 23.4 %collective-permute-done.2 = bf16[32,128,128]{2,1,0:T(8,128)(2,1)S(1)} collective-permute-done((bf16[32,128,128]{2,1,0:T(8,128)(2,1)S(1)}, bf16[32,128,128]{2,1,0:T(8,128)(2,1)S(1)}, u32[]{:S(2)}, u32[]{:S(2)}) %collective-permute-start.2) | collective-permute-done | bytes 1048608 | tf_op jit(solution)/shard_map/ppermute | solution.py:369
  290.3 0.0 collective-permute-done.1
  290.3 2.0 convert_add_fusion
  (3 shorter events, 0.0 us)
Async XLA Ops:
  2.0 190.6 %copy-start.1 = (bf16[32,128,128]{2,1,0:T(8,128)(2,1)S(1)}, bf16[32,128,128]{2,1,0:T(8,128)(2,1)}, u32[]{:S(2)}) copy-start(bf16[32,128,128]{2,1,0:T(8,128)(2,1)} %amp.3) | copy-start | bytes 3145732
  3.5 189.2 %copy-start.5 = (f32[8,128]{1,0:T(8,128)S(1)}, f32[8,128]{1,0:T(8,128)}, u32[]{:S(2)}) copy-start(f32[8,128]{1,0:T(8,128)} %maximum_bitcast_fusion.flts) | copy-start | bytes 12292
  4.9 187.8 %copy-start.4 = (s32[1024]{0:T(1024)S(1)}, s32[1024]{0:T(1024)}, u32[]{:S(2)}) copy-start(s32[1024]{0:T(1024)} %concatenate.6) | copy-start | bytes 12292
  192.7 2.2 copy-start
  194.9 1.9 copy-start.2
  196.8 0.8 copy-start.3
  197.6 0.7 copy-start.6
  241.2 25.8 %collective-permute-start = (bf16[32,128,128]{2,1,0:T(8,128)(2,1)S(1)}, bf16[32,128,128]{2,1,0:T(8,128)(2,1)S(1)}, u32[]{:S(2)}, u32[]{:S(2)}) collective-permute-start(bf16[32,128,128]{2,1,0:T(8,128)(2,1)S(1)} %get-tuple-element.23), channel_id=1, source_target_pairs={{0,2},{1,3},{2,4},{3,5},{4,6},{5,7},{6,0},{7,1},{8,10},{9,11},{10,... | collective-permute-start | bytes 3145736 | tf_op jit(solution)/shard_map/ppermute | solution.py:369
  241.3 49.1 %collective-permute-start.2 = (bf16[32,128,128]{2,1,0:T(8,128)(2,1)S(1)}, bf16[32,128,128]{2,1,0:T(8,128)(2,1)S(1)}, u32[]{:S(2)}, u32[]{:S(2)}) collective-permute-start(bf16[32,128,128]{2,1,0:T(8,128)(2,1)S(1)} %get-tuple-element.24), channel_id=1, source_target_pairs={{0,4},{1,5},{2,6},{3,7},{4,0},{5,1},{6,2},{7,3},{8,12},{9,13},{10,... | collective-permute-start | bytes 3145736 | tf_op jit(solution)/shard_map/ppermute | solution.py:369
  245.4 45.0 %collective-permute-start.1 = (bf16[32,128,128]{2,1,0:T(8,128)(2,1)S(1)}, bf16[32,128,128]{2,1,0:T(8,128)(2,1)S(1)}, u32[]{:S(2)}, u32[]{:S(2)}) collective-permute-start(bf16[32,128,128]{2,1,0:T(8,128)(2,1)S(1)} %get-tuple-element.25), channel_id=1, source_target_pairs={{0,6},{1,7},{2,0},{3,1},{4,2},{5,3},{6,4},{7,5},{8,14},{9,15},{10,... | collective-permute-start | bytes 3145736 | tf_op jit(solution)/shard_map/ppermute | solution.py:369

commit v2 on v0

v2 whole, which is shorter than its diff:
```python
import jax
import jax.numpy as jnp
from jax import lax
from jax.experimental import pallas as pl
from jax.experimental.pallas import tpu as pltpu
from jax.sharding import PartitionSpec as P

MESH = pl.DeviceIdType.MESH
BF = jnp.bfloat16
F32 = jnp.float32
I32 = jnp.int32
HALF = 16
PIECE = 8
MATE = 3
FAR, MATE_FAR = 2, 6
OWN = 7
PLUS = (0, 2, 3, 4)


def table_kernel(
    owner, pair, target, coef, c_owner, c_pair, c_target, c_coef, live, ints, flts, fill, c_fill
):
    def clear(i, carry):
        for r in (0, 1, 2, 4):
            ints[r, i] = 0
        flts[0, i] = 0.0
        flts[1, i] = 0.0
        return carry

    lax.fori_loop(0, 128, clear, 0)

    def clear_fill(i, carry):
        fill[i] = 0
        ints[3, i] = live[i]
        return carry

    lax.fori_loop(0, 32, clear_fill, 0)
    for i in range(4):
        c_fill[i] = 0

    def put(t, carry):
        o = owner[t]
        k = fill[o]
        fill[o] = k + 1
        e = o * 4 + k
        p = target[t]
        ints[0, e] = pair[t]
        ints[1, e] = p
        ints[2, e] = live[p]
        flts[0, e] = coef[t]
        return carry

    lax.fori_loop(0, 64, put, 0)

    def c_put(t, carry):
        o = c_owner[t]
        k = c_fill[o]
        c_fill[o] = k + 1
        e = o * 8 + k
        p = c_target[t]
        ints[4, e] = c_pair[t]
        ints[4, 32 + e] = p
        ints[4, 64 + e] = live[p]
        flts[1, e] = c_coef[t]
        return carry

    lax.fori_loop(0, 16, c_put, 0)


def tables(*lists):
    smem = pl.BlockSpec(memory_space=pltpu.SMEM)
    return pl.pallas_call(
        table_kernel,
        out_shape=[jax.ShapeDtypeStruct((8, 128), I32), jax.ShapeDtypeStruct((8, 128), F32)],
        in_specs=[smem] * 9,
        out_specs=[smem] * 2,
        scratch_shapes=[pltpu.SMEM((32,), I32), pltpu.SMEM((4,), I32)],
    )(*lists)


def main_kernel(
    pno, amp, ints, flts, mix,
    own_out, col_out, terms_in, relay_in, row_l, row_a, z_l, y_l, y_a, ints_in, flts_in,
    mix_v, met, chunk_l0, chunk_l1, chunk_a0, chunk_a1, far_l0, far_l1, far_a0, far_a1,
    terms, col_terms, met_buf, ints_s, flts_s, send_sem, recv_sem, load_sem, met_sem, out_sem,
):
    chunks = ((chunk_l0, chunk_a0), (chunk_l1, chunk_a1))
    far = ((far_l0, far_a0), (far_l1, far_a1))
    me = lax.axis_index("mem")
    g = lax.axis_index("grp")
    core = me % 2
    z = (me // 2) % 4
    x = me // 8

    def member(dx, dz, dc):
        return ((x + dx) % 4) * 8 + ((z + dz) % 4) * 2 + (core + dc) % 2

    def up(dg):
        return ((g + dg) % 4, me)

    row_m = [member(1, 0, 0), member(3, 0, 0), member(2, 0, 0), member(0, 0, 1),
             member(1, 0, 1), member(3, 0, 1), member(2, 0, 1), me]
    row = [(g, m) for m in row_m[:7]]
    col = [(g, member(0, d, 0)) for d in (1, 3, 2)]
    tall = [up(1), up(3), up(2)]
    back = (1, 0, 2, 3, 5, 4, 6)
    mate = row[MATE]

    barrier = pltpu.get_barrier_semaphore()
    peers = row + col + tall
    for d in peers:
        pl.semaphore_signal(barrier, inc=1, device_id=d, device_id_type=MESH)
    pl.semaphore_wait(barrier, len(peers))

    live = []
    arrived = set()

    def send(src, dst, dev):
        i = len(live)
        cp = pltpu.make_async_remote_copy(
            src_ref=src, dst_ref=dst, send_sem=send_sem.at[i], recv_sem=recv_sem.at[i],
            device_id=dev, device_id_type=MESH,
        )
        cp.start()
        live.append(cp)
        return cp

    def arrive(cps):
        for cp in cps:
            cp.wait_recv()
            arrived.add(id(cp))

    local = []

    def keep(src, dst):
        cp = pltpu.make_async_copy(src, dst, out_sem.at[len(local)])
        cp.start()
        local.append(cp)

    H1 = pl.ds(0, HALF)
    H2 = pl.ds(HALF, HALF)

    def own(dsts, srcs, devs):
        res = {}
        for way, order in ((0, (H2, H1)), (1, (H1, H2))):
            for n, h in enumerate(order):
                res[(1 - way, n)] = [
                    send(src.at[h], dst.at[1 - way, h], devs[way]) for src, dst in zip(srcs, dsts)
                ]
        return res

    riders = []
    for k, d in enumerate(row):
        riders.append(send(ints, ints_in.at[back[k]], d))
    for k, d in enumerate(col):
        riders.append(send(ints, ints_in.at[7 + back[k]], d))
        riders.append(send(flts, flts_in.at[back[k]], d))
    for k, d in enumerate(tall):
        riders.append(send(ints, ints_in.at[10 + back[k]], d))
    got_x = own([row_l, row_a], [pno, amp], row)
    got_z = own([z_l], [pno], col)
    got_y = own([y_l, y_a], [pno, amp], tall)
    got_mate = [send(pno, row_l.at[MATE], mate), send(amp, row_a.at[MATE], mate)]

    pltpu.sync_copy(mix, mix_v)

    def metric_of(src, zt):
        def load(i, b):
            return pltpu.make_async_copy(src.at[pl.ds(i * 4, 4)], met_buf.at[b], met_sem.at[b])

        load(0, 0).start()

        def step(i, carry):
            b = i % 2
            load(i, b).wait()

            @pl.when(i < 7)
            def _():
                load(i + 1, 1 - b).start()

            for u in (0, 2):
                two = jnp.concatenate([met_buf[b, u], met_buf[b, u + 1]], axis=1)
                mixed = jnp.dot(mix_v[...], two, preferred_element_type=F32)
                full = (two.astype(F32) + mixed).astype(BF)
                met[zt, i * 4 + u] = full[:, :128].T
                met[zt, i * 4 + u + 1] = full[:, 128:].T
            return carry

        lax.fori_loop(0, 8, step, 0)

    rows = lax.broadcasted_iota(I32, (128, 128), 0)
    lanes = lax.broadcasted_iota(I32, (128, 128), 1)

    def four(spots, lref, aref, store):
        inters, halves = [], []
        for zt, t, p, live_p, live_q, coef in spots:
            inter = jnp.dot(met[zt, t], lref[p], preferred_element_type=F32)
            ok = (rows < live_p) & (lanes < live_q)
            inters.append(jnp.where(ok, inter, 0.0).astype(BF))
        for (zt, t, p, live_p, live_q, coef), inter in zip(spots, inters):
            halves.append(jnp.dot(inter, aref[p], preferred_element_type=F32).astype(BF))
        for n, (spot, inter, half) in enumerate(zip(spots, inters, halves)):
            term = lax.dot_general(half, inter, (((1,), (1,)), ((), ())), preferred_element_type=F32)
            store(n, (-spot[5] * term).astype(BF))

    def row_slots(j, lref, aref, zt):
        spots = []
        for k in range(4):
            e = row_m[j] * 4 + k
            p = ints_s[7 + zt, 0, e]
            spots.append((zt, ints_s[7 + zt, 1, e], p, ints_s[7 + zt, 2, e], ints_s[j, 3, p],
                          flts_s[zt, 0, e]))

        def store(n, v):
            terms[zt, j, n] = v

        four(spots, lref, aref, store)

    def row_work(j, lref, aref, first, last):
        def step(zt, carry):
            row_slots(j, lref, aref, zt)
            return carry

        lax.fori_loop(first, last, step, 0)

    def col_work(rel, lref, aref):
        group = (g + (0, 1, 3, 2)[rel]) % 4
        src = OWN if rel == 0 else 10 + rel

        def step(q, carry):
            spots = []
            for n in range(4):
                e = group * 8 + q * 4 + n
                p = ints_s[7, 4, e]
                spots.append((0, ints_s[7, 4, 32 + e], p, ints_s[7, 4, 64 + e], ints_s[src, 3, p],
                              flts_s[0, 1, e]))

            def store(n, v):
                col_terms[rel, q * 4 + n] = v

            four(spots, lref, aref, store)
            return carry

        lax.fori_loop(0, 2, step, 0)
        keep(col_terms.at[rel], col_out.at[rel])

    passing = {}

    def give(j, zt):
        if zt == 0:
            keep(terms.at[0, j], own_out.at[j])
        elif zt == 3:
            way = 0 if j in PLUS else 1
            passing[j] = send(terms.at[3, j], relay_in.at[j], col[way])
        else:
            send(terms.at[zt, j], terms_in.at[back[zt - 1], j], col[zt - 1])

    def pass_on(j):
        arrive([passing[j]])
        send(relay_in.at[j], terms_in.at[2, j], col[0 if j in PLUS else 1])

    def blocks_of(j):
        if j == OWN:
            return pno, amp
        return row_l.at[j], row_a.at[j]

    def run(stages, late=()):
        def load(i, fn):
            b = i % 2
            for k, (src, dst) in enumerate(zip(stages[i][0], chunks[b])):
                getattr(pltpu.make_async_copy(src, dst, load_sem.at[b, k]), fn)()

        load(0, "start")
        gifts = list(late)
        for i, (blocks, work, after) in enumerate(stages):
            load(i, "wait")
            if i + 1 < len(stages):
                load(i + 1, "start")
            work(*chunks[i % 2])
            for j, zt in gifts:
                give(j, zt)
            gifts = after
        return gifts

    def row_stage(j, first, last):
        return (blocks_of(j), lambda l, a: row_work(j, l, a, first, last),
                [(j, zt) for zt in range(first, last)])

    def col_stage(rel):
        return (y_l.at[rel - 1], y_a.at[rel - 1]), lambda l, a: col_work(rel, l, a), []

    def relay(got, dsts, devs):
        out = []
        for slot, h, way in ((1, H2, 0), (0, H1, 1)):
            arrive(got[(slot, 0)])
            for dst in dsts:
                out.append(send(dst.at[slot, h], dst.at[2, h], devs[way]))
        return out

    metric_of(pno, 0)
    arrive(riders)
    pltpu.sync_copy(ints_in.at[pl.ds(0, 7)], ints_s.at[pl.ds(0, 7)])
    pltpu.sync_copy(ints, ints_s.at[7])
    pltpu.sync_copy(ints_in.at[pl.ds(7, 6)], ints_s.at[pl.ds(8, 6)])
    pltpu.sync_copy(flts, flts_s.at[0])
    pltpu.sync_copy(flts_in, flts_s.at[pl.ds(1, 3)])
    arrive(got_mate)

    def first_work(l, a):
        row_work(OWN, l, a, 0, 1)
        col_work(0, l, a)

    left = run([((pno, amp), first_work, [(OWN, 0)]), row_stage(MATE, 0, 1)])

    far_z = relay(got_z, [z_l], col)
    far_x = []
    for slot, h, way in ((1, H2, 0), (0, H1, 1)):
        arrive(got_x[(slot, 0)])
        for q in (0, 1):
            part = pl.ds((HALF if way == 0 else 0) + q * PIECE, PIECE)
            far_x.append((part, [
                send(row_l.at[slot, part], far_l0.at[part], row[way]),
                send(row_a.at[slot, part], far_a0.at[part], row[way]),
            ]))
    got_mx = []
    for slot, h in ((1, H2), (0, H1)):
        for dst in (row_l, row_a):
            got_mx.append(send(dst.at[slot, h], dst.at[4 + slot, h], mate))
    far_y = relay(got_y, [y_l, y_a], tall)

    for slot in (0, 1):
        arrive(got_z[(slot, 1)])
        metric_of(z_l.at[slot], 1 + slot)
    left = run([row_stage(OWN, 1, 3), row_stage(MATE, 1, 3)], left)
    for slot, h in ((1, H1), (0, H2)):
        arrive(got_x[(slot, 1)])
        for dst in (row_l, row_a):
            got_mx.append(send(dst.at[slot, h], dst.at[4 + slot, h], mate))
    left = run([row_stage(0, 0, 3), row_stage(1, 0, 3)], left)
    arrive(got_mx)
    for slot in (0, 1):
        arrive(got_y[(slot, 1)])
    left = run([row_stage(4, 0, 3), row_stage(5, 0, 3), col_stage(1), col_stage(2)], left)
    arrive(far_z)
    metric_of(z_l.at[2], 3)
    near = (OWN, MATE, 0, 1, 4, 5)
    left = run([row_stage(j, 3, 4) for j in near], left)
    for j in near[:-1]:
        pass_on(j)
    for j, zt in left:
        give(j, zt)
    pass_on(near[-1])

    mate_far = []
    for part, cps in (far_x[0], far_x[2], far_x[1], far_x[3]):
        arrive(cps)
        for src, dst in zip(*far):
            mate_far.append(send(src.at[part], dst.at[part], mate))
    for n, j in ((0, FAR), (1, MATE_FAR)):
        if n == 1:
            arrive(mate_far)
        row_slots(j, *far[n], 3)
        row_slots(j, *far[n], 1)
        give(j, 3)
        row_slots(j, *far[n], 2)
        give(j, 1)
        row_slots(j, *far[n], 0)
        give(j, 2)
    pass_on(FAR)
    give(FAR, 0)
    give(MATE_FAR, 0)
    pass_on(MATE_FAR)
    arrive(far_y)
    run([col_stage(3)])
    for cp in local:
        cp.wait()
    for cp in live:
        cp.wait_send()
        if id(cp) not in arrived:
            cp.wait_recv()


def main(pno, amp, ints, flts, mix):
    any_spec = pl.BlockSpec(memory_space=pl.ANY)
    shape = jax.ShapeDtypeStruct
    outs = [
        shape((8, 4, 128, 128), BF),
        shape((4, 8, 128, 128), BF),
        shape((3, 8, 4, 128, 128), BF),
        shape((8, 4, 128, 128), BF),
        shape((7, 32, 512, 128), BF),
        shape((7, 32, 128, 128), BF),
        shape((3, 32, 512, 128), BF),
        shape((3, 32, 512, 128), BF),
        shape((3, 32, 128, 128), BF),
        shape((13, 8, 128), I32),
        shape((3, 8, 128), F32),
    ]
    return pl.pallas_call(
        main_kernel,
        out_shape=outs,
        in_specs=[any_spec] * 5,
        out_specs=[any_spec] * len(outs),
        scratch_shapes=[
            pltpu.VMEM((512, 512), BF),
            pltpu.VMEM((4, 32, 128, 512), BF),
            pltpu.VMEM((32, 512, 128), BF),
            pltpu.VMEM((32, 512, 128), BF),
            pltpu.VMEM((32, 128, 128), BF),
            pltpu.VMEM((32, 128, 128), BF),
            pltpu.VMEM((32, 512, 128), BF),
            pltpu.VMEM((32, 512, 128), BF),
            pltpu.VMEM((32, 128, 128), BF),
            pltpu.VMEM((32, 128, 128), BF),
            pltpu.VMEM((4, 8, 4, 128, 128), BF),
            pltpu.VMEM((4, 8, 128, 128), BF),
            pltpu.VMEM((2, 4, 512, 128), BF),
            pltpu.SMEM((14, 8, 128), I32),
            pltpu.SMEM((4, 8, 128), F32),
            pltpu.SemaphoreType.DMA((128,)),
            pltpu.SemaphoreType.DMA((128,)),
            pltpu.SemaphoreType.DMA((2, 2)),
            pltpu.SemaphoreType.DMA((2,)),
            pltpu.SemaphoreType.DMA((16,)),
        ],
        compiler_params=pltpu.CompilerParams(
            collective_id=0, has_side_effects=True, vmem_limit_bytes=63 << 20
        ),
    )(pno, amp, ints, flts, mix)


def sum_kernel(ints, own_terms, col_terms, terms_in, out):
    me = lax.axis_index("mem")
    core = me % 2
    z = (me // 2) % 4
    x = me // 8
    out[...] = jnp.zeros_like(out)
    from_z = (0, 1, 3, 2)
    from_x = (1, 3, 2, 0, 1, 3, 2, 0)
    for j in range(8):
        for zi in range(4):
            m = ((x + from_x[j]) % 4) * 8 + ((z + from_z[zi]) % 4) * 2 + (core + (3 <= j < 7)) % 2
            for k in range(4):
                e = m * 4 + k

                @pl.when(ints[2, e] > 0)
                def _():
                    t = ints[1, e]
                    v = own_terms[j, k] if zi == 0 else terms_in[zi - 1, j, k]
                    out[t] = out[t] + v.astype(F32)

    g = lax.axis_index("grp")
    for rel in range(4):
        for k in range(8):
            e = ((g + (0, 1, 3, 2)[rel]) % 4) * 8 + k

            @pl.when(ints[4, 64 + e] > 0)
            def _():
                t = ints[4, 32 + e]
                out[t] = out[t] + col_terms[rel, k].astype(F32)


def total(ints, own_terms, col_terms, terms_in):
    vmem = pl.BlockSpec(memory_space=pltpu.VMEM)
    return pl.pallas_call(
        sum_kernel,
        out_shape=jax.ShapeDtypeStruct((32, 128, 128), F32),
        in_specs=[pl.BlockSpec(memory_space=pltpu.SMEM)] + [vmem] * 3,
        out_specs=vmem,
    )(ints, own_terms, col_terms, terms_in)


def shards(
    pno, amplitudes, pno_count, pao_coupling,
    row_owner, row_pair, row_target, row_coef,
    column_owner, column_pair, column_target, column_coef,
):
    ints, flts = tables(
        row_owner[:, 0], row_pair, row_target, row_coef,
        column_owner[:, 0], column_pair, column_target, column_coef, pno_count,
    )
    outs = main(pno, amplitudes, ints, flts, pao_coupling.T)
    return total(ints, *outs[:3])


def solution(mesh):
    both = P(("grp", "mem"))
    in_specs = (
        P(("grp", "mem"), None, None),
        P(("grp", "mem"), None, None),
        both,
        P(),
        P(("grp", "mem"), None),
        both,
        both,
        both,
        P(("grp", "mem"), None),
        both,
        both,
        both,
    )
    out_specs = P(("grp", "mem"), None, None)
    return jax.shard_map(shards, mesh=mesh, in_specs=in_specs, out_specs=out_specs, check_vma=False)
```

time: 497 us -> 215 us (0.43)
  the two profiles are of different devices: /device:TPU:36 before, /device:TPU:1 now
where the time goes in v2:
time: 215 us; the launch traced here: 213 us
  Pallas kernels  211 us (98%)
    pallas_call x1, Pallas kernels, main(): pl.pallas_call(main_kernel, out_shape=outs, in_specs=[any_spec] * 5, out_...  200 us
    pallas_call x1, Pallas kernels, total(): pl.pallas_call(sum_kernel, out_shape=jax.ShapeDtypeStruct((32, 128, 128),...  6.42 us

profile of v2, /device:TPU:1, one launch (start us, length us, event | category | flops | bytes accessed | tf_op | source)
XLA Modules:
  0.0 212.7 jit_solution(17118083178173275392)
XLA Ops:
  0.0 4.2 %shard_map.118 = (s32[8,128]{1,0:T(8,128)}, f32[8,128]{1,0:T(8,128)}) custom-call(s32[64]{0:T(128)} %bitcast.4, s32[64]{0:T(128)} %pair.1, s32[64]{0:T(128)} %target.1, f32[64]{0:T(128)} %coef.1, s32[16]{0:T(128)} %bitcast.5, s32[16]{0:T(128)} %c_pair.1, s32[16]{0:T(128)} %c_target.1, f32[16]{0:T(128)} %c_coef.1, s32[32]{0:T(128)} %live.1), custom_call_target="tpu_custom_call" | custom-call | tf_op jit(solution)/shard_map/pallas_call | solution.py:72
  4.2 2.0 copy.13
  6.2 200.0 %shard_map.119 = (bf16[8,4,128,128]{3,2,1,0:T(8,128)(2,1)}, bf16[4,8,128,128]{3,2,1,0:T(8,128)(2,1)}, bf16[3,8,4,128,128]{4,3,2,1,0:T(8,128)(2,1)}, bf16[8,4,128...) custom-call(bf16[32,512,128]{2,1,0:T(8,128)(2,1)} %pno.1, ...), custom_call_target="tpu_custom_call" | custom-call | tf_op jit(solution)/shard_map/pallas_call | solution.py:399
  206.3 6.4 %shard_map.120 = f32[32,128,128]{2,1,0:T(8,128)} custom-call(s32[8,128]{1,0:T(8,128)} %get-tuple-element.10.ints, bf16[8,4,128,128]{3,2,1,0:T(8,128)(2,1)} %get-tuple-element.12.own_terms, bf16[4,8,128,128]{3,2,1,0:T(8,128)(2,1)} %get-tuple-element.13.col_terms, bf16[3,8,4,128,128]{4,3,2,1,0:T(8,128)(2,1)} %get-tuple-element.14.terms_in), custom_call_target="tpu_custom_call" | custom-call | tf_op jit(solution)/shard_map/pallas_call | solution.py:465

commit v3 on v2

--- a/solution.py
+++ b/solution.py
@@ -17,73 +17,21 @@
 PLUS = (0, 2, 3, 4)
 
 
-def table_kernel(
-    owner, pair, target, coef, c_owner, c_pair, c_target, c_coef, live, ints, flts, fill, c_fill
+def main_kernel(
+    pno, amp, mix, *refs,
 ):
-    def clear(i, carry):
-        for r in (0, 1, 2, 4):
-            ints[r, i] = 0
-        flts[0, i] = 0.0
-        flts[1, i] = 0.0
-        return carry
-
-    lax.fori_loop(0, 128, clear, 0)
-
-    def clear_fill(i, carry):
-        fill[i] = 0
-        ints[3, i] = live[i]
-        return carry
-
-    lax.fori_loop(0, 32, clear_fill, 0)
-    for i in range(4):
-        c_fill[i] = 0
-
-    def put(t, carry):
-        o = owner[t]
-        k = fill[o]
-        fill[o] = k + 1
-        e = o * 4 + k
-        p = target[t]
-        ints[0, e] = pair[t]
-        ints[1, e] = p
-        ints[2, e] = live[p]
-        flts[0, e] = coef[t]
-        return carry
-
-    lax.fori_loop(0, 64, put, 0)
-
-    def c_put(t, carry):
-        o = c_owner[t]
-        k = c_fill[o]
-        c_fill[o] = k + 1
-        e = o * 8 + k
-        p = c_target[t]
-        ints[4, e] = c_pair[t]
-        ints[4, 32 + e] = p
-        ints[4, 64 + e] = live[p]
-        flts[1, e] = c_coef[t]
-        return carry
-
-    lax.fori_loop(0, 16, c_put, 0)
-
-
-def tables(*lists):
-    smem = pl.BlockSpec(memory_space=pltpu.SMEM)
-    return pl.pallas_call(
-        table_kernel,
-        out_shape=[jax.ShapeDtypeStruct((8, 128), I32), jax.ShapeDtypeStruct((8, 128), F32)],
-        in_specs=[smem] * 9,
-        out_specs=[smem] * 2,
-        scratch_shapes=[pltpu.SMEM((32,), I32), pltpu.SMEM((4,), I32)],
-    )(*lists)
-
-
-def main_kernel(
-    pno, amp, ints, flts, mix,
-    own_out, col_out, terms_in, relay_in, row_l, row_a, z_l, y_l, y_a, ints_in, flts_in,
-    mix_v, met, chunk_l0, chunk_l1, chunk_a0, chunk_a1, far_l0, far_l1, far_a0, far_a1,
-    terms, col_terms, met_buf, ints_s, flts_s, send_sem, recv_sem, load_sem, met_sem, out_sem,
-):
+    lists = refs[:9]
+    (
+        own_out, col_out, terms_in, ints, flts,
+        relay_in, row_l, row_a, z_l, y_l, y_a, ints_in, flts_in,
+    ) = refs[9:22]
+    list_v = refs[22:31]
+    (
+        wide, tab_i, tab_f, mix_in, mix_v, met,
+        chunk_l0, chunk_l1, chunk_a0, chunk_a1, far_l0, far_l1, far_a0, far_a1,
+        terms, col_terms, met_buf, ints_s, flts_s, send_sem, recv_sem, load_sem, met_sem,
+        out_sem, list_sem,
+    ) = refs[31:]
     chunks = ((chunk_l0, chunk_a0), (chunk_l1, chunk_a1))
     far = ((far_l0, far_a0), (far_l1, far_a1))
     me = lax.axis_index("mem")
@@ -149,6 +97,61 @@
                 ]
         return res
 
+    got_x = own([row_l, row_a], [pno, amp], row)
+    got_z = own([z_l], [pno], col)
+    got_y = own([y_l, y_a], [pno, amp], tall)
+    got_mate = [send(pno, row_l.at[MATE], mate), send(amp, row_a.at[MATE], mate)]
+
+    small = [
+        pltpu.make_async_copy(src, dst, list_sem.at[i])
+        for i, (src, dst) in enumerate(zip(lists + (mix,), list_v + (mix_in,)))
+    ]
+    for cp in small:
+        cp.start()
+    rows = lax.broadcasted_iota(I32, (128, 128), 0)
+    lanes = lax.broadcasted_iota(I32, (128, 128), 1)
+    wide[...] = jnp.zeros_like(wide)
+    for i, cp in enumerate(small[:9]):
+        cp.wait()
+        wide[i:i + 1, 0:list_v[i].shape[1]] = list_v[i][...].astype(F32)
+
+    def across(i):
+        return jnp.broadcast_to(wide[i:i + 1, :], (128, 128))
+
+    def down(i):
+        return across(i).T
+
+    def place(owner, first, number, room):
+        mine = down(owner)
+        same = (mine == across(owner)) & (lanes < rows) & (lanes < number)
+        earlier = jnp.sum(jnp.where(same, 1.0, 0.0), axis=1, keepdims=True)
+        slot = (mine * room + earlier).astype(I32)
+        target = down(first + 2)
+        kept = (target.astype(I32) == lanes) & (lanes < 32)
+        alive = jnp.sum(jnp.where(kept, across(4), 0.0), axis=1, keepdims=True)
+        return slot, (down(first + 1), target, jnp.broadcast_to(alive, (128, 128))), down(first + 3)
+
+    def spread(slot, number, shift, value):
+        hit = (slot + shift == lanes) & (rows < number)
+        return jnp.sum(jnp.where(hit, value, 0.0), axis=0, keepdims=True)
+
+    slot, parts, coef = place(0, 0, 64, 4)
+    tab_i[...] = jnp.zeros_like(tab_i)
+    tab_f[...] = jnp.zeros_like(tab_f)
+    for r, value in enumerate(parts):
+        tab_i[r:r + 1, :] = spread(slot, 64, 0, value).astype(I32)
+    tab_f[0:1, :] = spread(slot, 64, 0, coef)
+    tab_i[3:4, :] = wide[4:5, :].astype(I32)
+    slot, parts, coef = place(5, 5, 16, 8)
+    tab_i[4:5, :] = sum(
+        spread(slot, 16, 32 * r, value) for r, value in enumerate(parts)
+    ).astype(I32)
+    tab_f[1:2, :] = spread(slot, 16, 0, coef)
+    small[9].wait()
+    mix_v[...] = mix_in[...].T
+    pltpu.sync_copy(tab_i, ints)
+    pltpu.sync_copy(tab_f, flts)
+
     riders = []
     for k, d in enumerate(row):
         riders.append(send(ints, ints_in.at[back[k]], d))
@@ -157,12 +160,6 @@
         riders.append(send(flts, flts_in.at[back[k]], d))
     for k, d in enumerate(tall):
         riders.append(send(ints, ints_in.at[10 + back[k]], d))
-    got_x = own([row_l, row_a], [pno, amp], row)
-    got_z = own([z_l], [pno], col)
-    got_y = own([y_l, y_a], [pno, amp], tall)
-    got_mate = [send(pno, row_l.at[MATE], mate), send(amp, row_a.at[MATE], mate)]
-
-    pltpu.sync_copy(mix, mix_v)
 
     def metric_of(src, zt):
         def load(i, b):
@@ -187,9 +184,6 @@
             return carry
 
         lax.fori_loop(0, 8, step, 0)
-
-    rows = lax.broadcasted_iota(I32, (128, 128), 0)
-    lanes = lax.broadcasted_iota(I32, (128, 128), 1)
 
     def four(spots, lref, aref, store):
         inters, halves = [], []
@@ -207,8 +201,8 @@
         spots = []
         for k in range(4):
             e = row_m[j] * 4 + k
-            p = ints_s[7 + zt, 0, e]
-            spots.append((zt, ints_s[7 + zt, 1, e], p, ints_s[7 + zt, 2, e], ints_s[j, 3, p],
+            p = ints_s[7 + zt, 0, e] & 31
+            spots.append((zt, ints_s[7 + zt, 1, e] & 31, p, ints_s[7 + zt, 2, e], ints_s[j, 3, p],
                           flts_s[zt, 0, e]))
 
         def store(n, v):
@@ -231,8 +225,8 @@
             spots = []
             for n in range(4):
                 e = group * 8 + q * 4 + n
-                p = ints_s[7, 4, e]
-                spots.append((0, ints_s[7, 4, 32 + e], p, ints_s[7, 4, 64 + e], ints_s[src, 3, p],
+                p = ints_s[7, 4, e] & 31
+                spots.append((0, ints_s[7, 4, 32 + e] & 31, p, ints_s[7, 4, 64 + e], ints_s[src, 3, p],
                               flts_s[0, 1, e]))
 
             def store(n, v):
@@ -380,13 +374,15 @@
             cp.wait_recv()
 
 
-def main(pno, amp, ints, flts, mix):
+def main(pno, amp, mix, lists):
     any_spec = pl.BlockSpec(memory_space=pl.ANY)
     shape = jax.ShapeDtypeStruct
     outs = [
         shape((8, 4, 128, 128), BF),
         shape((4, 8, 128, 128), BF),
         shape((3, 8, 4, 128, 128), BF),
+        shape((8, 128), I32),
+        shape((8, 128), F32),
         shape((8, 4, 128, 128), BF),
         shape((7, 32, 512, 128), BF),
         shape((7, 32, 128, 128), BF),
@@ -399,9 +395,13 @@
     return pl.pallas_call(
         main_kernel,
         out_shape=outs,
-        in_specs=[any_spec] * 5,
+        in_specs=[any_spec] * 12,
         out_specs=[any_spec] * len(outs),
-        scratch_shapes=[
+        scratch_shapes=[pltpu.VMEM(v.shape, v.dtype) for v in lists] + [
+            pltpu.VMEM((16, 128), F32),
+            pltpu.VMEM((8, 128), I32),
+            pltpu.VMEM((8, 128), F32),
+            pltpu.VMEM((512, 512), BF),
             pltpu.VMEM((512, 512), BF),
             pltpu.VMEM((4, 32, 128, 512), BF),
             pltpu.VMEM((32, 512, 128), BF),
@@ -422,23 +422,32 @@
             pltpu.SemaphoreType.DMA((2, 2)),
             pltpu.SemaphoreType.DMA((2,)),
             pltpu.SemaphoreType.DMA((16,)),
+            pltpu.SemaphoreType.DMA((10,)),
         ],
         compiler_params=pltpu.CompilerParams(
             collective_id=0, has_side_effects=True, vmem_limit_bytes=63 << 20
         ),
-    )(pno, amp, ints, flts, mix)
-
-
-def sum_kernel(ints, own_terms, col_terms, terms_in, out):
+    )(pno, amp, mix, *lists)
+
+
+def sum_kernel(ints, own_terms, col_terms, terms_in, out, own_v, col_v, in_v, sem):
     me = lax.axis_index("mem")
+    g = lax.axis_index("grp")
     core = me % 2
     z = (me // 2) % 4
     x = me // 8
+    loads = [
+        pltpu.make_async_copy(own_terms, own_v, sem.at[0]),
+        pltpu.make_async_copy(col_terms, col_v, sem.at[1]),
+    ] + [pltpu.make_async_copy(terms_in.at[i], in_v.at[i], sem.at[2 + i]) for i in range(3)]
+    for cp in loads:
+        cp.start()
     out[...] = jnp.zeros_like(out)
     from_z = (0, 1, 3, 2)
     from_x = (1, 3, 2, 0, 1, 3, 2, 0)
-    for j in range(8):
-        for zi in range(4):
+    for zi in range(4):
+        loads[zi + 1 if zi else 0].wait()
+        for j in range(8):
             m = ((x + from_x[j]) % 4) * 8 + ((z + from_z[zi]) % 4) * 2 + (core + (3 <= j < 7)) % 2
             for k in range(4):
                 e = m * 4 + k
@@ -446,27 +455,35 @@
                 @pl.when(ints[2, e] > 0)
                 def _():
                     t = ints[1, e]
-                    v = own_terms[j, k] if zi == 0 else terms_in[zi - 1, j, k]
+                    v = own_v[j, k] if zi == 0 else in_v[zi - 1, j, k]
                     out[t] = out[t] + v.astype(F32)
 
-    g = lax.axis_index("grp")
-    for rel in range(4):
-        for k in range(8):
-            e = ((g + (0, 1, 3, 2)[rel]) % 4) * 8 + k
-
-            @pl.when(ints[4, 64 + e] > 0)
-            def _():
-                t = ints[4, 32 + e]
-                out[t] = out[t] + col_terms[rel, k].astype(F32)
+        if zi == 0:
+            loads[1].wait()
+            for rel in range(4):
+                for k in range(8):
+                    e = ((g + (0, 1, 3, 2)[rel]) % 4) * 8 + k
+
+                    @pl.when(ints[4, 64 + e] > 0)
+                    def _():
+                        t = ints[4, 32 + e]
+                        out[t] = out[t] + col_v[rel, k].astype(F32)
 
 
 def total(ints, own_terms, col_terms, terms_in):
-    vmem = pl.BlockSpec(memory_space=pltpu.VMEM)
+    any_spec = pl.BlockSpec(memory_space=pl.ANY)
     return pl.pallas_call(
         sum_kernel,
         out_shape=jax.ShapeDtypeStruct((32, 128, 128), F32),
-        in_specs=[pl.BlockSpec(memory_space=pltpu.SMEM)] + [vmem] * 3,
-        out_specs=vmem,
+        in_specs=[pl.BlockSpec(memory_space=pltpu.SMEM)] + [any_spec] * 3,
+        out_specs=pl.BlockSpec(memory_space=pltpu.VMEM),
+        scratch_shapes=[
+            pltpu.VMEM(own_terms.shape, BF),
+            pltpu.VMEM(col_terms.shape, BF),
+            pltpu.VMEM(terms_in.shape, BF),
+            pltpu.SemaphoreType.DMA((5,)),
+        ],
+        compiler_params=pltpu.CompilerParams(vmem_limit_bytes=63 << 20),
     )(ints, own_terms, col_terms, terms_in)
 
 
@@ -475,12 +492,15 @@
     row_owner, row_pair, row_target, row_coef,
     column_owner, column_pair, column_target, column_coef,
 ):
-    ints, flts = tables(
-        row_owner[:, 0], row_pair, row_target, row_coef,
-        column_owner[:, 0], column_pair, column_target, column_coef, pno_count,
-    )
-    outs = main(pno, amplitudes, ints, flts, pao_coupling.T)
-    return total(ints, *outs[:3])
+    lists = [
+        v.reshape(1, -1)
+        for v in (
+            row_owner, row_pair, row_target, row_coef, pno_count,
+            column_owner, column_pair, column_target, column_coef,
+        )
+    ]
+    own_terms, col_terms, terms_in, ints = main(pno, amplitudes, pao_coupling, lists)[:4]
+    return total(ints, own_terms, col_terms, terms_in)
 
 
 def solution(mesh):

time: 215 us -> 246 us (1.14)
  Pallas kernels: 211 us -> 244 us
    pallas_call x2 -> x1, Pallas kernels: 204 us -> 238 us  [main(): pl.pallas_call(main_kernel, out_shape=outs, in_specs=[any_spec] * 12, out...]
where the time goes in v3:
time: 246 us; the launch traced here: 244 us
  Pallas kernels  244 us (99%)
    pallas_call x1, Pallas kernels, main(): pl.pallas_call(main_kernel, out_shape=outs, in_specs=[any_spec] * 12, out...  238 us
    pallas_call x1, Pallas kernels, total(): pl.pallas_call(sum_kernel, out_shape=jax.ShapeDtypeStruct((32, 128, 128),...  5.71 us

profile of v3, /device:TPU:1, one launch (start us, length us, event | category | flops | bytes accessed | tf_op | source)
XLA Modules:
  0.0 243.9 jit_solution(17380272858267629800)
XLA Ops:
  0.0 238.0 %shard_map.118 = (bf16[8,4,128,128]{3,2,1,0:T(8,128)(2,1)}, bf16[4,8,128,128]{3,2,1,0:T(8,128)(2,1)}, bf16[3,8,4,128,128]{4,3,2,1,0:T(8,128)(2,1)}, s32[8,128]{1...) custom-call(bf16[32,512,128]{2,1,0:T(8,128)(2,1)} %pno.1, ...), custom_call_target="tpu_custom_call" | custom-call | tf_op jit(solution)/shard_map/pallas_call | solution.py:395
  238.0 5.7 %shard_map.119 = f32[32,128,128]{2,1,0:T(8,128)} custom-call(s32[8,128]{1,0:T(8,128)} %get-tuple-element.9.ints, bf16[8,4,128,128]{3,2,1,0:T(8,128)(2,1)} %get-tuple-element.10.own_terms, bf16[4,8,128,128]{3,2,1,0:T(8,128)(2,1)} %get-tuple-element.11.col_terms, bf16[3,8,4,128,128]{4,3,2,1,0:T(8,128)(2,1)} %get-tuple-element.12.terms_in), custom_call_target="tpu_custom_call" | custom-call | tf_op jit(solution)/shard_map/pallas_call | solution.py:475

commit v4 on v3

--- a/solution.py
+++ b/solution.py
@@ -54,12 +54,6 @@
     back = (1, 0, 2, 3, 5, 4, 6)
     mate = row[MATE]
 
-    barrier = pltpu.get_barrier_semaphore()
-    peers = row + col + tall
-    for d in peers:
-        pl.semaphore_signal(barrier, inc=1, device_id=d, device_id_type=MESH)
-    pl.semaphore_wait(barrier, len(peers))
-
     live = []
     arrived = set()
 
@@ -97,11 +91,10 @@
                 ]
         return res
 
-    got_x = own([row_l, row_a], [pno, amp], row)
-    got_z = own([z_l], [pno], col)
-    got_y = own([y_l, y_a], [pno, amp], tall)
-    got_mate = [send(pno, row_l.at[MATE], mate), send(amp, row_a.at[MATE], mate)]
-
+    barrier = pltpu.get_barrier_semaphore()
+    peers = row + col + tall
+    for d in peers:
+        pl.semaphore_signal(barrier, inc=1, device_id=d, device_id_type=MESH)
     small = [
         pltpu.make_async_copy(src, dst, list_sem.at[i])
         for i, (src, dst) in enumerate(zip(lists + (mix,), list_v + (mix_in,)))
@@ -147,11 +140,15 @@
         spread(slot, 16, 32 * r, value) for r, value in enumerate(parts)
     ).astype(I32)
     tab_f[1:2, :] = spread(slot, 16, 0, coef)
-    small[9].wait()
-    mix_v[...] = mix_in[...].T
-    pltpu.sync_copy(tab_i, ints)
-    pltpu.sync_copy(tab_f, flts)
-
+    saves = [
+        pltpu.make_async_copy(tab_i, ints, list_sem.at[0]),
+        pltpu.make_async_copy(tab_f, flts, list_sem.at[1]),
+    ]
+    for cp in saves:
+        cp.start()
+    pl.semaphore_wait(barrier, len(peers))
+    for cp in saves:
+        cp.wait()
     riders = []
     for k, d in enumerate(row):
         riders.append(send(ints, ints_in.at[back[k]], d))
@@ -160,6 +157,12 @@
         riders.append(send(flts, flts_in.at[back[k]], d))
     for k, d in enumerate(tall):
         riders.append(send(ints, ints_in.at[10 + back[k]], d))
+    got_x = own([row_l, row_a], [pno, amp], row)
+    got_z = own([z_l], [pno], col)
+    got_y = own([y_l, y_a], [pno, amp], tall)
+    got_mate = [send(pno, row_l.at[MATE], mate), send(amp, row_a.at[MATE], mate)]
+    small[9].wait()
+    mix_v[...] = mix_in[...].T
 
     def metric_of(src, zt):
         def load(i, b):

time: 246 us -> 208 us (0.85)
  Pallas kernels: 244 us -> 206 us
    pallas_call x1, Pallas kernels: 238 us -> 200 us  [main(): pl.pallas_call(main_kernel, out_shape=outs, in_specs=[any_spec] * 12, out...]
where the time goes in v4:
time: 208 us; the launch traced here: 206 us
  Pallas kernels  206 us (99%)
    pallas_call x1, Pallas kernels, main(): pl.pallas_call(main_kernel, out_shape=outs, in_specs=[any_spec] * 12, out...  200 us
    pallas_call x1, Pallas kernels, total(): pl.pallas_call(sum_kernel, out_shape=jax.ShapeDtypeStruct((32, 128, 128),...  5.71 us

profile of v4, /device:TPU:1, one launch (start us, length us, event | category | flops | bytes accessed | tf_op | source)
XLA Modules:
  0.0 206.0 jit_solution(2002258407354243719)
XLA Ops:
  0.0 200.1 %shard_map.118 = (bf16[8,4,128,128]{3,2,1,0:T(8,128)(2,1)}, bf16[4,8,128,128]{3,2,1,0:T(8,128)(2,1)}, bf16[3,8,4,128,128]{4,3,2,1,0:T(8,128)(2,1)}, s32[8,128]{1...) custom-call(bf16[32,512,128]{2,1,0:T(8,128)(2,1)} %pno.1, ...), custom_call_target="tpu_custom_call" | custom-call | tf_op jit(solution)/shard_map/pallas_call | solution.py:398
  200.1 5.7 %shard_map.119 = f32[32,128,128]{2,1,0:T(8,128)} custom-call(s32[8,128]{1,0:T(8,128)} %get-tuple-element.9.ints, bf16[8,4,128,128]{3,2,1,0:T(8,128)(2,1)} %get-tuple-element.10.own_terms, bf16[4,8,128,128]{3,2,1,0:T(8,128)(2,1)} %get-tuple-element.11.col_terms, bf16[3,8,4,128,128]{4,3,2,1,0:T(8,128)(2,1)} %get-tuple-element.12.terms_in), custom_call_target="tpu_custom_call" | custom-call | tf_op jit(solution)/shard_map/pallas_call | solution.py:478

commit v5 on v4

--- a/solution.py
+++ b/solution.py
@@ -28,7 +28,7 @@
     list_v = refs[22:31]
     (
         wide, tab_i, tab_f, mix_in, mix_v, met,
-        chunk_l0, chunk_l1, chunk_a0, chunk_a1, far_l0, far_l1, far_a0, far_a1,
+        own_l, own_a, mate_l, mate_a, chunk_l0, chunk_l1, chunk_a0, chunk_a1, far_l0, far_l1, far_a0, far_a1,
         terms, col_terms, met_buf, ints_s, flts_s, send_sem, recv_sem, load_sem, met_sem,
         out_sem, list_sem,
     ) = refs[31:]
@@ -160,7 +160,13 @@
     got_x = own([row_l, row_a], [pno, amp], row)
     got_z = own([z_l], [pno], col)
     got_y = own([y_l, y_a], [pno, amp], tall)
-    got_mate = [send(pno, row_l.at[MATE], mate), send(amp, row_a.at[MATE], mate)]
+    got_mate = [send(pno, mate_l, mate), send(amp, mate_a, mate)]
+    home = [
+        pltpu.make_async_copy(pno, own_l, list_sem.at[2]),
+        pltpu.make_async_copy(amp, own_a, list_sem.at[3]),
+    ]
+    for cp in home:
+        cp.start()
     small[9].wait()
     mix_v[...] = mix_in[...].T
 
@@ -257,30 +263,39 @@
         send(relay_in.at[j], terms_in.at[2, j], col[0 if j in PLUS else 1])
 
     def blocks_of(j):
-        if j == OWN:
-            return pno, amp
+        if j in (OWN, MATE):
+            return None
         return row_l.at[j], row_a.at[j]
 
     def run(stages, late=()):
+        loads = [n for n, stage in enumerate(stages) if stage[0] is not None]
+
         def load(i, fn):
             b = i % 2
-            for k, (src, dst) in enumerate(zip(stages[i][0], chunks[b])):
+            for k, (src, dst) in enumerate(zip(stages[loads[i]][0], chunks[b])):
                 getattr(pltpu.make_async_copy(src, dst, load_sem.at[b, k]), fn)()
 
-        load(0, "start")
+        if loads:
+            load(0, "start")
         gifts = list(late)
-        for i, (blocks, work, after) in enumerate(stages):
-            load(i, "wait")
-            if i + 1 < len(stages):
-                load(i + 1, "start")
-            work(*chunks[i % 2])
+        for n, (blocks, work, after) in enumerate(stages):
+            if blocks is None:
+                work(None, None)
+            else:
+                i = loads.index(n)
+                load(i, "wait")
+                if i + 1 < len(loads):
+                    load(i + 1, "start")
+                work(*chunks[i % 2])
             for j, zt in gifts:
                 give(j, zt)
             gifts = after
         return gifts
 
+    stay = {OWN: (own_l, own_a), MATE: (mate_l, mate_a)}
+
     def row_stage(j, first, last):
-        return (blocks_of(j), lambda l, a: row_work(j, l, a, first, last),
+        return (blocks_of(j), lambda l, a: row_work(j, *stay.get(j, (l, a)), first, last),
                 [(j, zt) for zt in range(first, last)])
 
     def col_stage(rel):
@@ -304,10 +319,13 @@
     arrive(got_mate)
 
     def first_work(l, a):
-        row_work(OWN, l, a, 0, 1)
-        col_work(0, l, a)
-
-    left = run([((pno, amp), first_work, [(OWN, 0)]), row_stage(MATE, 0, 1)])
+        row_work(OWN, own_l, own_a, 0, 1)
+        col_work(0, own_l, own_a)
+
+    for cp in home:
+        cp.wait()
+
+    left = run([(None, first_work, [(OWN, 0)]), row_stage(MATE, 0, 1)])
 
     far_z = relay(got_z, [z_l], col)
     far_x = []
@@ -408,6 +426,10 @@
             pltpu.VMEM((512, 512), BF),
             pltpu.VMEM((4, 32, 128, 512), BF),
             pltpu.VMEM((32, 512, 128), BF),
+            pltpu.VMEM((32, 128, 128), BF),
+            pltpu.VMEM((32, 512, 128), BF),
+            pltpu.VMEM((32, 128, 128), BF),
+            pltpu.VMEM((32, 512, 128), BF),
             pltpu.VMEM((32, 512, 128), BF),
             pltpu.VMEM((32, 128, 128), BF),
             pltpu.VMEM((32, 128, 128), BF),

time: 208 us -> 204 us (0.981)
  Pallas kernels: 206 us -> 202 us
    pallas_call x1, Pallas kernels: 200 us -> 196 us  [main(): pl.pallas_call(main_kernel, out_shape=outs, in_specs=[any_spec] * 12, out...]
where the time goes in v5:
time: 204 us; the launch traced here: 202 us
  Pallas kernels  202 us (99%)
    pallas_call x1, Pallas kernels, main(): pl.pallas_call(main_kernel, out_shape=outs, in_specs=[any_spec] * 12, out...  196 us
    pallas_call x1, Pallas kernels, total(): pl.pallas_call(sum_kernel, out_shape=jax.ShapeDtypeStruct((32, 128, 128),...  5.71 us

profile of v5, /device:TPU:1, one launch (start us, length us, event | category | flops | bytes accessed | tf_op | source)
XLA Modules:
  0.0 202.4 jit_solution(17859507375409776675)
XLA Ops:
  0.0 196.5 %shard_map.118 = (bf16[8,4,128,128]{3,2,1,0:T(8,128)(2,1)}, bf16[4,8,128,128]{3,2,1,0:T(8,128)(2,1)}, bf16[3,8,4,128,128]{4,3,2,1,0:T(8,128)(2,1)}, s32[8,128]{1...) custom-call(bf16[32,512,128]{2,1,0:T(8,128)(2,1)} %pno.1, ...), custom_call_target="tpu_custom_call" | custom-call | tf_op jit(solution)/shard_map/pallas_call | solution.py:416
  196.5 5.7 %shard_map.119 = f32[32,128,128]{2,1,0:T(8,128)} custom-call(s32[8,128]{1,0:T(8,128)} %get-tuple-element.9.ints, bf16[8,4,128,128]{3,2,1,0:T(8,128)(2,1)} %get-tuple-element.10.own_terms, bf16[4,8,128,128]{3,2,1,0:T(8,128)(2,1)} %get-tuple-element.11.col_terms, bf16[3,8,4,128,128]{4,3,2,1,0:T(8,128)(2,1)} %get-tuple-element.12.terms_in), custom_call_target="tpu_custom_call" | custom-call | tf_op jit(solution)/shard_map/pallas_call | solution.py:500

commit v6 on v5

--- a/solution.py
+++ b/solution.py
@@ -342,6 +342,14 @@
         for dst in (row_l, row_a):
             got_mx.append(send(dst.at[slot, h], dst.at[4 + slot, h], mate))
     far_y = relay(got_y, [y_l, y_a], tall)
+    mate_far = []
+
+    def push(q):
+        for way in (0, 1):
+            part, cps = far_x[way * 2 + q]
+            arrive(cps)
+            for src, dst in zip(*far):
+                mate_far.append(send(src.at[part], dst.at[part], mate))
 
     for slot in (0, 1):
         arrive(got_z[(slot, 1)])
@@ -360,17 +368,14 @@
     metric_of(z_l.at[2], 3)
     near = (OWN, MATE, 0, 1, 4, 5)
     left = run([row_stage(j, 3, 4) for j in near], left)
+    push(0)
     for j in near[:-1]:
         pass_on(j)
     for j, zt in left:
         give(j, zt)
     pass_on(near[-1])
 
-    mate_far = []
-    for part, cps in (far_x[0], far_x[2], far_x[1], far_x[3]):
-        arrive(cps)
-        for src, dst in zip(*far):
-            mate_far.append(send(src.at[part], dst.at[part], mate))
+    push(1)
     for n, j in ((0, FAR), (1, MATE_FAR)):
         if n == 1:
             arrive(mate_far)

time: 204 us -> 204 us (level)
  no operation moved by 1% of the time
where the time goes in v6:
time: 204 us; the launch traced here: 202 us
  Pallas kernels  201 us (99%)
    pallas_call x1, Pallas kernels, main(): pl.pallas_call(main_kernel, out_shape=outs, in_specs=[any_spec] * 12, out...  196 us
    pallas_call x1, Pallas kernels, total(): pl.pallas_call(sum_kernel, out_shape=jax.ShapeDtypeStruct((32, 128, 128),...  5.71 us

profile of v6, /device:TPU:1, one launch (start us, length us, event | category | flops | bytes accessed | tf_op | source)
XLA Modules:
  0.0 201.6 jit_solution(8640069124918894318)
XLA Ops:
  0.0 195.8 %shard_map.118 = (bf16[8,4,128,128]{3,2,1,0:T(8,128)(2,1)}, bf16[4,8,128,128]{3,2,1,0:T(8,128)(2,1)}, bf16[3,8,4,128,128]{4,3,2,1,0:T(8,128)(2,1)}, s32[8,128]{1...) custom-call(bf16[32,512,128]{2,1,0:T(8,128)(2,1)} %pno.1, ...), custom_call_target="tpu_custom_call" | custom-call | tf_op jit(solution)/shard_map/pallas_call | solution.py:421
  195.8 5.7 %shard_map.119 = f32[32,128,128]{2,1,0:T(8,128)} custom-call(s32[8,128]{1,0:T(8,128)} %get-tuple-element.9.ints, bf16[8,4,128,128]{3,2,1,0:T(8,128)(2,1)} %get-tuple-element.10.own_terms, bf16[4,8,128,128]{3,2,1,0:T(8,128)(2,1)} %get-tuple-element.11.col_terms, bf16[3,8,4,128,128]{4,3,2,1,0:T(8,128)(2,1)} %get-tuple-element.12.terms_in), custom_call_target="tpu_custom_call" | custom-call | tf_op jit(solution)/shard_map/pallas_call | solution.py:505
